TPU v7x, 128 devices: a whole 4x4x4 slice. The times are simulated.
128 devices in a mesh: gx: 8 (over x, core), gy: 16 (over z, y).
Axes of the slice: x: 4, y: 4, z: 4, core: 2. Of those that a mesh axis runs over, the one named last changes fastest.
Arguments:
- parent_fields: float32 [5, 4, 384, 6144], P(None, None, 'gx', 'gy'), may hold values from -6 to 6
- parent_velocity: float32 [2, 4, 384, 6144], P(None, None, 'gx', 'gy'), may hold values from -0.3 to 0.3
- parent_mixing: float32 [4, 384, 6144], P(None, 'gx', 'gy'), may hold values from 0.01 to 0.1
- nest_fields: float32 [5, 4, 384, 6144], P(None, None, 'gx', 'gy'), may hold values from -6 to 6
- nest_velocity: float32 [2, 4, 384, 6144], P(None, None, 'gx', 'gy'), may hold values from -0.3 to 0.3
- nest_mixing: float32 [4, 384, 6144], P(None, 'gx', 'gy'), may hold values from 0.01 to 0.1
- nest_anchor: int32 [2], replicated, may hold values from 1 to 3327, as said below
Outputs:
- parent_result: float32 [5, 4, 384, 6144], P(None, None, 'gx', 'gy')
- nest_result: float32 [5, 4, 384, 6144], P(None, None, 'gx', 'gy')
Inputs may be any that keep to these rules, and one draw needn't show every extreme that they name: `nest_anchor`: the row anchor is 1 to 254; the column anchor is 3073 to 3327, so the nest with a rim of one parent cell lies inside the parent grid.
All inputs are finite; a program needn't handle non-finite values.
Results may differ from a plain program's by a relative error of at most 0.00002.
Values sent between devices are 32-bit elements; how exact they have to be, the bound alone decides.
A program may use at most 192 MiB of HBM per device.

v0:
```python
import jax
import jax.numpy as jnp
from jax import lax
from jax.sharding import PartitionSpec as P

SUBSTEPS = 3
third = 1.0 / 3.0
two_thirds = 2.0 / 3.0
nudge_floor = 0.1
relax_width = 4.0


def extended(cells, sides, width):
    for axis, dim in sides:
        count = lax.axis_size(axis)
        ends = count - 1
        head = lax.slice_in_dim(cells, 0, width, axis=dim)
        tail = lax.slice_in_dim(cells, cells.shape[dim] - width, cells.shape[dim], axis=dim)
        cells = jnp.concatenate(
            [
                lax.ppermute(tail, axis, [(i, (i + 1) % count) for i in range(ends)]),
                cells,
                lax.ppermute(head, axis, [((i + 1) % count, i) for i in range(ends)]),
            ],
            axis=dim,
        )
    return cells


def update(values, padded, velocity, mixing):
    western = padded[:, :, :-2, 1:-1]
    eastern = padded[:, :, 2:, 1:-1]
    southern = padded[:, :, 1:-1, :-2]
    northern = padded[:, :, 1:-1, 2:]
    along_rows = velocity[0]
    along_columns = velocity[1]
    upwind = (
        jnp.maximum(along_rows, 0.0) * (values - western)
        + jnp.minimum(along_rows, 0.0) * (eastern - values)
        + jnp.maximum(along_columns, 0.0) * (values - southern)
        + jnp.minimum(along_columns, 0.0) * (northern - values)
    )
    return values - upwind + mixing * (eastern + western + northern + southern - 4.0 * values)


def refine_rows(block):
    lower = block[:, :, :-2]
    centre = block[:, :, 1:-1]
    upper = block[:, :, 2:]
    stacked = jnp.stack(
        (third * lower + two_thirds * centre, centre, two_thirds * centre + third * upper), axis=3
    )
    extent = centre.shape
    return stacked.reshape(extent[0], extent[1], 3 * extent[2], extent[3])


def refine_columns(block):
    lower = block[:, :, :, :-2]
    centre = block[:, :, :, 1:-1]
    upper = block[:, :, :, 2:]
    stacked = jnp.stack(
        (third * lower + two_thirds * centre, centre, two_thirds * centre + third * upper), axis=4
    )
    extent = centre.shape
    return stacked.reshape(extent[0], extent[1], extent[2], 3 * extent[3])


def block_mean(state):
    extent = state.shape
    grouped = state.reshape(extent[0], extent[1], extent[2] // 3, 3, extent[3] // 3, 3)
    return jnp.sum(grouped, axis=(3, 5)) / 9.0


def relax_weight(row_global, column_global, total_rows, total_columns):
    row_distance = jnp.minimum(row_global, total_rows - 1 - row_global)
    column_distance = jnp.minimum(column_global, total_columns - 1 - column_global)
    distance = jnp.minimum(row_distance[:, None], column_distance[None, :]).astype(jnp.float32)
    return nudge_floor + (1.0 - nudge_floor) * jnp.exp(-distance / relax_width)


def take_rows(values, positions, valid):
    picked = jnp.take(values, jnp.clip(positions, 0, values.shape[2] - 1), axis=2)
    return jnp.where(valid[:, None], picked, 0.0)


def take_columns(values, positions, valid):
    picked = jnp.take(values, jnp.clip(positions, 0, values.shape[3] - 1), axis=3)
    return jnp.where(valid, picked, 0.0)


def within(positions, limit):
    return (positions >= 0) & (positions < limit)


def spans(anchor, count, length):
    offsets = (
        jnp.arange(count, dtype=jnp.int32)[:, None] * length
        + jnp.arange(length + 2, dtype=jnp.int32)[None, :]
    )
    return anchor - 1 + offsets.reshape(-1)


def owner_mask(owners, count):
    return (owners[None, :] == jnp.arange(count, dtype=jnp.int32)[:, None]).reshape(-1)


def spread_rows(values, owners, count):
    tiled = jnp.tile(values, (1, 1, count, 1))
    return jnp.where(owner_mask(owners, count)[:, None], tiled, 0.0)


def spread_columns(values, owners, count):
    tiled = jnp.tile(values, (1, 1, 1, count))
    return jnp.where(owner_mask(owners, count), tiled, 0.0)


def per_device(
    parent_fields,
    parent_velocity,
    parent_mixing,
    nest_fields,
    nest_velocity,
    nest_mixing,
    nest_anchor,
):
    row_rank = lax.axis_index("gx")
    column_rank = lax.axis_index("gy")
    row_devices = lax.axis_size("gx")
    column_devices = lax.axis_size("gy")
    fields_count = parent_fields.shape[0]
    levels_count = parent_fields.shape[1]
    parent_rows = parent_fields.shape[2]
    parent_columns = parent_fields.shape[3]
    nest_rows = nest_fields.shape[2]
    nest_columns = nest_fields.shape[3]
    span_rows = nest_rows // 3
    span_columns = nest_columns // 3
    row_anchor = nest_anchor[0]
    column_anchor = nest_anchor[1]
    parent_padded = extended(parent_fields, (("gx", 2), ("gy", 3)), 1)
    parent_next = update(parent_fields, parent_padded, parent_velocity, parent_mixing)
    row_targets = spans(row_anchor, row_devices, span_rows) - row_rank * parent_rows
    column_targets = (
        spans(column_anchor, column_devices, span_columns) - column_rank * parent_columns
    )
    outgoing = take_columns(parent_next, column_targets, within(column_targets, parent_columns))
    incoming = lax.all_to_all(outgoing, "gy", split_axis=3, concat_axis=3, tiled=True)
    partial_block = incoming.reshape(
        fields_count, levels_count, parent_rows, column_devices, span_columns + 2
    ).sum(axis=3)
    outgoing_rows = take_rows(partial_block, row_targets, within(row_targets, parent_rows))
    incoming_rows = lax.all_to_all(outgoing_rows, "gx", split_axis=2, concat_axis=2, tiled=True)
    relay = incoming_rows.reshape(
        fields_count, levels_count, row_devices, span_rows + 2, span_columns + 2
    ).sum(axis=2)
    forcing = refine_columns(refine_rows(relay))
    row_global = row_rank * nest_rows + jnp.arange(nest_rows, dtype=jnp.int32)
    column_global = column_rank * nest_columns + jnp.arange(nest_columns, dtype=jnp.int32)
    weight = relax_weight(
        row_global, column_global, row_devices * nest_rows, column_devices * nest_columns
    )
    state = nest_fields
    for substep in range(SUBSTEPS):
        nest_padded = extended(state, (("gx", 2), ("gy", 3)), 1)
        moved = update(state, nest_padded, nest_velocity, nest_mixing)
        state = moved + weight * (forcing - moved)
    coarse = block_mean(state)
    own_rows = row_anchor + row_rank * span_rows + jnp.arange(span_rows, dtype=jnp.int32)
    own_columns = (
        column_anchor + column_rank * span_columns + jnp.arange(span_columns, dtype=jnp.int32)
    )
    relative_rows = row_rank * parent_rows + jnp.arange(parent_rows, dtype=jnp.int32) - row_anchor
    relative_columns = (
        column_rank * parent_columns + jnp.arange(parent_columns, dtype=jnp.int32) - column_anchor
    )
    rows_valid = within(relative_rows, row_devices * span_rows)
    columns_valid = within(relative_columns, column_devices * span_columns)
    outgoing = spread_columns(coarse, own_columns // parent_columns, column_devices)
    incoming = lax.all_to_all(outgoing, "gy", split_axis=3, concat_axis=3, tiled=True)
    placed = take_columns(incoming, relative_columns, columns_valid)
    outgoing_rows = spread_rows(placed, own_rows // parent_rows, row_devices)
    incoming_rows = lax.all_to_all(outgoing_rows, "gx", split_axis=2, concat_axis=2, tiled=True)
    fed_back = take_rows(incoming_rows, relative_rows, rows_valid)
    covered = rows_valid[:, None] & columns_valid[None, :]
    parent_result = jnp.where(covered, fed_back, parent_next)
    return (parent_result, state)


def solution(mesh):
    placed = (
        P(None, None, "gx", "gy"),
        P(None, None, "gx", "gy"),
        P(None, "gx", "gy"),
        P(None, None, "gx", "gy"),
        P(None, None, "gx", "gy"),
        P(None, "gx", "gy"),
        P(),
    )
    return jax.shard_map(
        per_device,
        mesh=mesh,
        in_specs=placed,
        out_specs=(P(None, None, "gx", "gy"), P(None, None, "gx", "gy")),
        check_vma=False,
    )
```

profile of v0, /device:TPU:1, one launch (start us, length us, event | category | flops | bytes accessed | tf_op | source)
XLA Modules:
  0.0 732.8 jit_solution(10386896655536340189)
XLA Ops:
  29.8 32.2 %gather_fusion = f32[2080,5,4,48]{3,2,1,0:T(4,128)} fusion(f32[5,4,48,384]{2,1,3,0:T(4,128)} %copy.257, s32[3072]{0:T(1024)S(1)} %copy-done.19), kind=kCustom, calls=%fused_computation | custom fusion | bytes 15982720 | tf_op jit(solution)/shard_map/jit(_take)/gather | solution.py:87
  62.0 15.2 %fusion.87 = f32[2080,5,4,48]{3,2,1,0:T(4,128)} fusion(f32[2080,5,4,48]{3,2,1,0:T(4,128)} %gather_fusion, pred[2080]{0:T(1024)(128)(4,1)S(1)} %copy-done.21, pred[2080]{0:T(1024)(128)(4,1)S(1)} %copy-done.20), kind=kLoop, calls=%fused_computation.195 | loop fusion | flops 3993600 | bytes 15978560
  77.2 26.0 %reshape.359 = f32[16,1,124800]{2,1,0:T(1,128)} reshape(f32[2080,5,4,48]{3,2,1,0:T(4,128)} %fusion.87) | data formatting | bytes 15974400
  103.2 9.4 %all-to-all-start = ((f32[16,1,124800]{2,1,0:T(1,128)}), f32[16,1,124800]{2,1,0:T(1,128)}, u32[]{:S(2)}, u32[]{:S(2)}) async-start(f32[16,1,124800]{2,1,0:T(1,128)} %reshape.359), calls=%async_computation | async-start | bytes 15974400 | tf_op jit(solution)/shard_map/all_to_all | solution.py:147
  113.7 120.9 %all-to-all-done = f32[16,1,124800]{2,1,0:T(1,128)} async-done(((f32[16,1,124800]{2,1,0:T(1,128)}), f32[16,1,124800]{2,1,0:T(1,128)}, u32[]{:S(2)}, u32[]{:S(2)}) %all-to-all-start) | async-done | bytes 7987232 | tf_op jit(solution)/shard_map/all_to_all | solution.py:147
  235.2 24.6 %reduce.4 = f32[16,124800]{1,0:T(8,128)} reduce(f32[16,1,124800]{2,1,0:T(1,128)} %all-to-all-done, f32[]{:T(128)} %broadcast.601), dimensions={1}, to_apply=%all_to_all.12.reduce_sub_computation | reduce | bytes 15974404 | tf_op jit(solution)/shard_map/all_to_all | solution.py:147
  259.8 28.8 %reshape.360 = f32[2080,5,4,48]{3,2,1,0:T(4,128)} reshape(f32[16,124800]{1,0:T(8,128)} %reduce.4) | data formatting | bytes 15974400
  288.6 11.8 %reduce_sum.27 = f32[5,4,48,130]{2,1,0,3:T(4,128)S(1)} reduce(f32[5,4,48,16,130]{2,1,0,4,3:T(4,128)} %bitcast.60, f32[]{:T(128)} %constant.66.clone.1), dimensions={3}, to_apply=%region_0.1 | reduce | flops 1872000 | bytes 8486404 | tf_op jit(solution)/shard_map/reduce_sum | solution.py:150
  322.7 24.9 %collective-permute-done = f32[5,4,1,384]{3,1,2,0:T(4,128)S(1)} collective-permute-done((f32[5,4,1,384]{3,1,2,0:T(4,128)S(1)}, f32[5,4,1,384]{3,1,2,0:T(4,128)S(1)}, u32[]{:S(2)}, u32[]{:S(2)}) %collective-permute-start) | collective-permute-done | bytes 30752 | tf_op jit(solution)/shard_map/ppermute | solution.py:21
  389.9 5.7 multiply_add_fusion.1
  406.9 6.1 collective-permute-start.14
  426.0 61.8 %reshape.322 = f32[5,4,16,3,128,3]{5,4,3,2,1,0:T(8,128)} reshape(f32[5,4,48,384]{3,2,1,0:T(8,128)} %multiply_add_fusion) | data formatting | bytes 2949120 | tf_op jit(solution)/shard_map/reshape | solution.py:70
  487.7 20.5 %reduce_sum.29 = f32[5,4,16,128]{3,2,1,0:T(8,128)S(1)} reduce(f32[5,4,16,3,128,3]{5,4,3,2,1,0:T(8,128)} %reshape.322, f32[]{:T(128)} %constant.66.clone.1), dimensions={3,5}, to_apply=%region_2.3 | reduce | flops 327680 | bytes 1638404 | tf_op jit(solution)/shard_map/reduce_sum | solution.py:71
  508.7 11.5 %bitcast_select_fusion = f32[5,4,16,2048]{2,1,0,3:T(4,128)} fusion(f32[5,4,16,128]{2,1,0,3:T(4,128)S(1)} %copy.286, pred[2048]{0:T(1024)(128)(4,1)S(1)} %fusion.70), kind=kLoop, calls=%fused_computation.5 | loop fusion | flops 655360 | bytes 2787328 | tf_op jit(solution)/shard_map/jit(_where)/select_n | solution.py:114
  520.2 21.1 %reshape.361 = f32[16,1,40960]{2,1,0:T(1,128)} reshape(f32[2048,5,4,16]{3,2,1,0:T(4,128)} %bitcast.61) | data formatting | bytes 5242880
  541.3 8.1 %all-to-all-start.2 = ((f32[16,1,40960]{2,1,0:T(1,128)}), f32[16,1,40960]{2,1,0:T(1,128)S(1)}, u32[]{:S(2)}, u32[]{:S(2)}) async-start(f32[16,1,40960]{2,1,0:T(1,128)} %reshape.361), calls=%async_computation.2 | async-start | bytes 5242880 | tf_op jit(solution)/shard_map/all_to_all | solution.py:179
  552.3 39.2 %all-to-all-done.2 = f32[16,1,40960]{2,1,0:T(1,128)S(1)} async-done(((f32[16,1,40960]{2,1,0:T(1,128)}), f32[16,1,40960]{2,1,0:T(1,128)S(1)}, u32[]{:S(2)}, u32[]{:S(2)}) %all-to-all-start.2) | async-done | bytes 2621472 | tf_op jit(solution)/shard_map/all_to_all | solution.py:179
  591.5 9.1 %reduce.5 = f32[16,40960]{1,0:T(8,128)} reduce(f32[16,1,40960]{2,1,0:T(1,128)S(1)} %all-to-all-done.2, f32[]{:T(128)} %broadcast.601), dimensions={1}, to_apply=%all_to_all.14.reduce_sub_computation | reduce | bytes 5242884 | tf_op jit(solution)/shard_map/all_to_all | solution.py:179
  600.6 25.4 %reshape.362 = f32[2048,5,4,16]{3,2,1,0:T(4,128)} reshape(f32[16,40960]{1,0:T(8,128)} %reduce.5) | data formatting | bytes 5242880
  626.0 17.1 %copy.287 = f32[5,4,16,2048]{2,1,3,0:T(4,128)} copy(f32[5,4,16,2048]{2,1,0,3:T(4,128)} %bitcast.62) | data formatting | bytes 5242880 | tf_op jit(solution)/shard_map/all_to_all | solution.py:179
  643.1 12.3 %gather_fusion.2 = f32[384,5,4,16]{3,2,1,0:T(4,128)} fusion(f32[5,4,16,2048]{2,1,3,0:T(4,128)} %copy.287, s32[1024]{0:T(1024)S(1)} %pad_clamp_fusion.2), kind=kCustom, calls=%fused_computation.2 | custom fusion | bytes 984576 | tf_op jit(solution)/shard_map/jit(_take)/gather | solution.py:87
  655.4 5.9 select_bitcast_fusion.1
  667.6 5.3 all-to-all-start.3
  676.1 42.9 %all-to-all-done.3 = f32[5,4,128,384]{3,1,0,2:T(4,128)} async-done(((f32[5,4,128,384]{3,1,0,2:T(4,128)}), f32[5,4,128,384]{3,1,0,2:T(4,128)}, u32[]{:S(2)}, u32[]{:S(2)}) %all-to-all-start.3) | async-done | bytes 3932192 | tf_op jit(solution)/shard_map/all_to_all | solution.py:182
  (178 shorter events, 142.4 us)
Async XLA Ops:
  0.6 13.0 %copy-start = (f32[5,4,48,384]{3,2,1,0:T(8,128)S(1)}, f32[5,4,48,384]{3,2,1,0:T(8,128)}, u32[]{:S(2)}) copy-start(f32[5,4,48,384]{3,2,1,0:T(8,128)} %param.7) | copy-start | bytes 4423684
  1.9 11.7 %collective-permute-start.4 = (f32[5,4,1,384]{3,1,2,0:T(4,128)S(1)}, f32[5,4,1,384]{3,1,2,0:T(4,128)S(1)}, u32[]{:S(2)}, u32[]{:S(2)}) collective-permute-start(f32[5,4,1,384]{3,1,2,0:T(4,128)S(1)} %copy.294), channel_id=1, source_target_pairs={{0,16},{16,32},{32,48},{48,64},{64,80},{80,96},{96,112},{1,17},{17... | collective-permute-start | bytes 92168 | tf_op jit(solution)/shard_map/ppermute | solution.py:21
  6.4 7.2 collective-permute-start.5
  14.3 6.1 collective-permute-start.6
  17.7 4.4 collective-permute-start.7
  29.8 32.2 %copy-start.20 = (pred[2080]{0:T(1024)(128)(4,1)S(1)}, pred[2080]{0:T(1024)(128)(4,1)}, u32[]{:S(2)}) copy-start(pred[2080]{0:T(1024)(128)(4,1)} %reshape.324) | copy-start | bytes 6244
  29.8 32.2 %copy-start.21 = (pred[2080]{0:T(1024)(128)(4,1)S(1)}, pred[2080]{0:T(1024)(128)(4,1)}, u32[]{:S(2)}) copy-start(pred[2080]{0:T(1024)(128)(4,1)} %compare_and_fusion) | copy-start | bytes 6244
  103.2 131.5 %all-to-all-start = ((f32[16,1,124800]{2,1,0:T(1,128)}), f32[16,1,124800]{2,1,0:T(1,128)}, u32[]{:S(2)}, u32[]{:S(2)}) async-start(f32[16,1,124800]{2,1,0:T(1,128)} %reshape.359), calls=%async_computation | async-start | bytes 15974400 | tf_op jit(solution)/shard_map/all_to_all | solution.py:147
  310.5 49.5 %all-to-all-start.1 = ((f32[5,4,144,130]{3,1,0,2:T(4,128)}), f32[5,4,144,130]{3,1,0,2:T(4,128)S(1)}, u32[]{:S(2)}, u32[]{:S(2)}) async-start(f32[5,4,144,130]{3,1,0,2:T(4,128)} %select_bitcast_fusion.2), calls=%async_computation.1 | async-start | bytes 5898240 | tf_op jit(solution)/shard_map/all_to_all | solution.py:152
  314.8 34.8 %copy-start.3 = (f32[5,4,48,384]{3,2,1,0:T(8,128)S(1)}, f32[5,4,48,384]{3,2,1,0:T(8,128)}, u32[]{:S(2)}) copy-start(f32[5,4,48,384]{3,2,1,0:T(8,128)} %param.10) | copy-start | bytes 4423684
  316.1 31.5 %collective-permute-start = (f32[5,4,1,384]{3,1,2,0:T(4,128)S(1)}, f32[5,4,1,384]{3,1,2,0:T(4,128)S(1)}, u32[]{:S(2)}, u32[]{:S(2)}) collective-permute-start(f32[5,4,1,384]{3,1,2,0:T(4,128)S(1)} %copy.292), channel_id=1, source_target_pairs={{0,16},{16,32},{32,48},{48,64},{64,80},{80,96},{96,112},{1,17},{17... | collective-permute-start | bytes 92168 | tf_op jit(solution)/shard_map/ppermute | solution.py:21
  319.7 30.0 %collective-permute-start.1 = (f32[5,4,1,384]{3,1,2,0:T(4,128)S(1)}, f32[5,4,1,384]{3,1,2,0:T(4,128)S(1)}, u32[]{:S(2)}, u32[]{:S(2)}) collective-permute-start(f32[5,4,1,384]{3,1,2,0:T(4,128)S(1)} %copy.293), channel_id=1, source_target_pairs={{16,0},{32,16},{48,32},{64,48},{80,64},{96,80},{112,96},{17,1},{33... | collective-permute-start | bytes 92168 | tf_op jit(solution)/shard_map/ppermute | solution.py:23
  352.1 4.2 collective-permute-start.2
  354.2 4.6 collective-permute-start.3
  373.1 5.5 collective-permute-start.8
  376.6 5.2 collective-permute-start.9
  382.5 3.9 collective-permute-start.10
  384.4 4.4 collective-permute-start.11
  395.7 5.8 collective-permute-start.12
  399.0 5.2 collective-permute-start.13
  406.9 9.9 %collective-permute-start.14 = (f32[5,4,50,1]{2,1,3,0:T(4,128)S(1)}, f32[5,4,50,1]{2,1,3,0:T(4,128)}, u32[]{:S(2)}, u32[]{:S(2)}) collective-permute-start(f32[5,4,50,1]{2,1,3,0:T(4,128)S(1)} %copy.281), channel_id=1, source_target_pairs={{0,1},{1,2},{2,3},{3,4},{4,5},{5,6},{6,7},{7,8},{8,9},{9,10},{10,1... | collective-permute-start | bytes 12008 | tf_op jit(solution)/shard_map/ppermute | solution.py:21
  414.9 4.7 collective-permute-start.15
  541.3 50.2 %all-to-all-start.2 = ((f32[16,1,40960]{2,1,0:T(1,128)}), f32[16,1,40960]{2,1,0:T(1,128)S(1)}, u32[]{:S(2)}, u32[]{:S(2)}) async-start(f32[16,1,40960]{2,1,0:T(1,128)} %reshape.361), calls=%async_computation.2 | async-start | bytes 5242880 | tf_op jit(solution)/shard_map/all_to_all | solution.py:179
  667.6 51.4 %all-to-all-start.3 = ((f32[5,4,128,384]{3,1,0,2:T(4,128)}), f32[5,4,128,384]{3,1,0,2:T(4,128)}, u32[]{:S(2)}, u32[]{:S(2)}) async-start(f32[5,4,128,384]{3,1,0,2:T(4,128)} %bitcast_select_fusion.1), calls=%async_computation.3 | async-start | bytes 7864320 | tf_op jit(solution)/shard_map/all_to_all | solution.py:182
  (19 other events, 75.4 us)
where the time goes:
time: 743 us; the launch traced here: 733 us
  local copies, waits for them, and re-layouts  276 us (37%)
  waiting for transfers between devices  241 us (32%)
  other arithmetic  144 us (19%)
  starting transfers between devices  67.1 us (9%)
    all_to_all x2, waiting for transfers between devices, per_device(): lax.all_to_all(outgoing, 'gy', split_axis=3, concat_axis=3, tiled=True)  160 us
    unnamed x54, local copies, waits for them, and re-layouts  102 us
    reshape x1, local copies, waits for them, and re-layouts, block_mean(): state.reshape(extent[0], extent[1], extent[2] // 3, 3, extent[3] // 3, 3)  61.8 us
    gather x2, local copies, waits for them, and re-layouts, take_columns(): jnp.take(values, jnp.clip(positions, 0, values.shape[3] - 1), axis=3)  44.5 us
    all_to_all x2, waiting for transfers between devices, per_device(): lax.all_to_all(outgoing_rows, 'gx', split_axis=2, concat_axis=2, tiled=True)  42.9 us
    all_to_all x2, other arithmetic, per_device(): lax.all_to_all(outgoing, 'gy', split_axis=3, concat_axis=3, tiled=True)  33.8 us
    ppermute x8, starting transfers between devices, extended(): lax.ppermute(tail, axis, [(i, (i + 1) % count) for i in range(ends)])  27.1 us
    ppermute x8, waiting for transfers between devices, extended(): lax.ppermute(tail, axis, [(i, (i + 1) % count) for i in range(ends)])  24.9 us
  transfers between devices with their start and end apart: 20, of which 11 were waited for; matrix products, arithmetic and copies ran while one was open for 4% of the time, Pallas kernels for 0%

commit v1 on v0

--- a/solution.py
+++ b/solution.py
@@ -176,7 +176,10 @@
     rows_valid = within(relative_rows, row_devices * span_rows)
     columns_valid = within(relative_columns, column_devices * span_columns)
     outgoing = spread_columns(coarse, own_columns // parent_columns, column_devices)
-    incoming = lax.all_to_all(outgoing, "gy", split_axis=3, concat_axis=3, tiled=True)
+    size = lax.axis_size("gy")
+    blocks = jnp.stack(jnp.split(outgoing, size, axis=3), axis=0)
+    blocks = lax.all_to_all(blocks, "gy", split_axis=0, concat_axis=0)
+    incoming = jnp.concatenate(blocks, axis=3)
     placed = take_columns(incoming, relative_columns, columns_valid)
     outgoing_rows = spread_rows(placed, own_rows // parent_rows, row_devices)
     incoming_rows = lax.all_to_all(outgoing_rows, "gx", split_axis=2, concat_axis=2, tiled=True)

time: 743 us -> 707 us (0.952)
  local copies, waits for them, and re-layouts: 276 us -> 248 us
    all_to_all x0 -> x1, waiting for transfers between devices: none -> 40.5 us  [per_device(): blocks = lax.all_to_all(blocks, 'gy', split_axis=0, concat_axis=0)]
    all_to_all x2 -> x1, waiting for transfers between devices: 160 us -> 120 us  [per_device(): lax.all_to_all(outgoing, 'gy', split_axis=3, concat_axis=3, tiled=True)]
    unnamed x54 -> x53, local copies, waits for them, and re-layouts: 102 us -> 65.2 us
    all_to_all x2 -> x1, local copies, waits for them, and re-layouts: 17.7 us -> 0.51 us  [per_device(): lax.all_to_all(outgoing, 'gy', split_axis=3, concat_axis=3, tiled=True)]
    reshape x0 -> x1, local copies, waits for them, and re-layouts: none -> 14.8 us  [per_device(): incoming = jnp.concatenate(blocks, axis=3)]
    select_n x1, other arithmetic: 11.5 us -> 1.94 us  [spread_columns(): return jnp.where(owner_mask(owners, count), tiled, 0.0)]
    all_to_all x2 -> x1, other arithmetic: 33.8 us -> 24.7 us  [per_device(): lax.all_to_all(outgoing, 'gy', split_axis=3, concat_axis=3, tiled=True)]
    all_to_all x0 -> x1, starting transfers between devices: none -> 8.93 us  [per_device(): blocks = lax.all_to_all(blocks, 'gy', split_axis=0, concat_axis=0)]
  transfers between devices with their start and end apart: 20 -> 20, of which waited for: 11 -> 11; matrix products, arithmetic and copies ran while one was open for 4% -> 5% of each run, Pallas kernels for 0% -> 0%
where the time goes in v1:
time: 707 us; the launch traced here: 696 us
  local copies, waits for them, and re-layouts  248 us (35%)
  waiting for transfers between devices  239 us (34%)
  other arithmetic  137 us (19%)
  starting transfers between devices  68.8 us (10%)
    all_to_all x1, waiting for transfers between devices, per_device(): lax.all_to_all(outgoing, 'gy', split_axis=3, concat_axis=3, tiled=True)  120 us
    unnamed x53, local copies, waits for them, and re-layouts  65.2 us
    reshape x1, local copies, waits for them, and re-layouts, block_mean(): state.reshape(extent[0], extent[1], extent[2] // 3, 3, extent[3] // 3, 3)  61.7 us
    gather x2, local copies, waits for them, and re-layouts, take_columns(): jnp.take(values, jnp.clip(positions, 0, values.shape[3] - 1), axis=3)  44.7 us
    all_to_all x2, waiting for transfers between devices, per_device(): lax.all_to_all(outgoing_rows, 'gx', split_axis=2, concat_axis=2, tiled=True)  42.9 us
    all_to_all x1, waiting for transfers between devices, per_device(): blocks = lax.all_to_all(blocks, 'gy', split_axis=0, concat_axis=0)  40.5 us
    ppermute x8, starting transfers between devices, extended(): lax.ppermute(tail, axis, [(i, (i + 1) % count) for i in range(ends)])  27 us
    all_to_all x1, other arithmetic, per_device(): lax.all_to_all(outgoing, 'gy', split_axis=3, concat_axis=3, tiled=True)  24.7 us
  transfers between devices with their start and end apart: 20, of which 11 were waited for; matrix products, arithmetic and copies ran while one was open for 5% of the time, Pallas kernels for 0%

profile of v1, /device:TPU:1, one launch (start us, length us, event | category | flops | bytes accessed | tf_op | source)
XLA Modules:
  0.0 696.4 jit_solution(14712670385526613144)
XLA Ops:
  29.5 32.3 %gather_fusion = f32[2080,5,4,48]{3,2,1,0:T(4,128)} fusion(f32[5,4,48,384]{2,1,3,0:T(4,128)} %copy.273, s32[3072]{0:T(1024)} %pad_clamp_fusion), kind=kCustom, calls=%fused_computation | custom fusion | bytes 15982720 | tf_op jit(solution)/shard_map/jit(_take)/gather | solution.py:87
  61.9 15.2 %fusion.103 = f32[2080,5,4,48]{3,2,1,0:T(4,128)} fusion(f32[2080,5,4,48]{3,2,1,0:T(4,128)} %gather_fusion, pred[2080]{0:T(1024)(128)(4,1)S(1)} %copy-done.12, pred[2080]{0:T(1024)(128)(4,1)S(1)} %copy-done.11), kind=kLoop, calls=%fused_computation.227 | loop fusion | flops 3993600 | bytes 15978560
  77.0 26.0 %reshape.367 = f32[16,1,124800]{2,1,0:T(1,128)} reshape(f32[2080,5,4,48]{3,2,1,0:T(4,128)} %fusion.103) | data formatting | bytes 15974400
  103.0 9.8 %all-to-all-start = ((f32[16,1,124800]{2,1,0:T(1,128)}), f32[16,1,124800]{2,1,0:T(1,128)}, u32[]{:S(2)}, u32[]{:S(2)}) async-start(f32[16,1,124800]{2,1,0:T(1,128)} %reshape.367), calls=%async_computation | async-start | bytes 15974400 | tf_op jit(solution)/shard_map/all_to_all | solution.py:147
  115.0 119.8 %all-to-all-done = f32[16,1,124800]{2,1,0:T(1,128)} async-done(((f32[16,1,124800]{2,1,0:T(1,128)}), f32[16,1,124800]{2,1,0:T(1,128)}, u32[]{:S(2)}, u32[]{:S(2)}) %all-to-all-start) | async-done | bytes 7987232 | tf_op jit(solution)/shard_map/all_to_all | solution.py:147
  235.3 24.7 %reduce.4 = f32[16,124800]{1,0:T(8,128)} reduce(f32[16,1,124800]{2,1,0:T(1,128)} %all-to-all-done, f32[]{:T(128)} %broadcast.601), dimensions={1}, to_apply=%all_to_all.12.reduce_sub_computation | reduce | bytes 15974404 | tf_op jit(solution)/shard_map/all_to_all | solution.py:147
  260.0 28.8 %reshape.368 = f32[2080,5,4,48]{3,2,1,0:T(4,128)} reshape(f32[16,124800]{1,0:T(8,128)} %reduce.4) | data formatting | bytes 15974400
  288.8 12.9 %reduce_sum.27 = f32[5,4,48,130]{2,1,0,3:T(4,128)} reduce(f32[5,4,48,16,130]{2,1,0,4,3:T(4,128)} %bitcast.124, f32[]{:T(128)} %constant.66.clone.1), dimensions={3}, to_apply=%region_0.1 | reduce | flops 1872000 | bytes 8486404 | tf_op jit(solution)/shard_map/reduce_sum | solution.py:150
  312.4 5.1 all-to-all-start.1
  326.3 24.0 %collective-permute-done = f32[5,4,1,384]{3,1,2,0:T(4,128)S(1)} collective-permute-done((f32[5,4,1,384]{3,1,2,0:T(4,128)S(1)}, f32[5,4,1,384]{3,1,2,0:T(4,128)S(1)}, u32[]{:S(2)}, u32[]{:S(2)}) %collective-permute-start) | collective-permute-done | bytes 30752 | tf_op jit(solution)/shard_map/ppermute | solution.py:21
  374.2 5.7 multiply_add_fusion.2
  403.3 5.6 multiply_add_fusion.1
  433.9 6.6 multiply_add_fusion
  440.5 61.7 %reshape.328 = f32[5,4,16,3,128,3]{5,4,3,2,1,0:T(8,128)} reshape(f32[5,4,48,384]{3,2,1,0:T(8,128)} %multiply_add_fusion) | data formatting | bytes 2949120 | tf_op jit(solution)/shard_map/reshape | solution.py:70
  502.2 20.5 %reduce_sum.29 = f32[5,4,16,128]{3,2,1,0:T(8,128)S(1)} reduce(f32[5,4,16,3,128,3]{5,4,3,2,1,0:T(8,128)} %reshape.328, f32[]{:T(128)} %constant.66.clone.1), dimensions={3,5}, to_apply=%region_2.3 | reduce | flops 327680 | bytes 1638404 | tf_op jit(solution)/shard_map/reduce_sum | solution.py:71
  541.1 8.9 %all-to-all-start.2 = ((f32[16,5,4,16,128]{4,3,2,1,0:T(8,128)}), f32[16,5,4,16,128]{4,3,2,1,0:T(8,128)}, u32[]{:S(2)}, u32[]{:S(2)}) async-start(f32[16,5,4,16,128]{4,3,2,1,0:T(8,128)} %fusion.65), calls=%async_computation.2 | async-start | bytes 5242880 | tf_op jit(solution)/shard_map/all_to_all | solution.py:181
  551.9 40.5 %all-to-all-done.2 = f32[16,5,4,16,128]{4,3,2,1,0:T(8,128)} async-done(((f32[16,5,4,16,128]{4,3,2,1,0:T(8,128)}), f32[16,5,4,16,128]{4,3,2,1,0:T(8,128)}, u32[]{:S(2)}, u32[]{:S(2)}) %all-to-all-start.2) | async-done | bytes 2621472 | tf_op jit(solution)/shard_map/all_to_all | solution.py:181
  592.4 14.8 %copy.308 = f32[5,4,16,16,128]{2,1,4,3,0:T(4,128)} copy(f32[5,4,16,16,128]{4,2,1,0,3:T(8,128)} %bitcast.40) | data formatting | bytes 5242880 | tf_op jit(solution)/shard_map/reshape | solution.py:182
  607.2 12.3 %gather_fusion.2 = f32[384,5,4,16]{3,2,1,0:T(4,128)} fusion(f32[5,4,16,2048]{2,1,3,0:T(4,128)} %bitcast.125, s32[1024]{0:T(1024)S(1)} %copy-done.13), kind=kCustom, calls=%fused_computation.2 | custom fusion | bytes 984576 | tf_op jit(solution)/shard_map/jit(_take)/gather | solution.py:87
  619.6 6.0 select_bitcast_fusion.1
  631.8 5.2 all-to-all-start.3
  640.1 42.9 %all-to-all-done.3 = f32[5,4,128,384]{3,1,0,2:T(4,128)} async-done(((f32[5,4,128,384]{3,1,0,2:T(4,128)}), f32[5,4,128,384]{3,1,0,2:T(4,128)}, u32[]{:S(2)}, u32[]{:S(2)}) %all-to-all-start.3) | async-done | bytes 3932192 | tf_op jit(solution)/shard_map/all_to_all | solution.py:185
  683.0 4.7 copy.305
  691.5 4.6 bitcast_select_fusion.1
  (177 shorter events, 154.1 us)
Async XLA Ops:
  0.6 12.9 %copy-start = (f32[5,4,48,384]{3,2,1,0:T(8,128)S(1)}, f32[5,4,48,384]{3,2,1,0:T(8,128)}, u32[]{:S(2)}) copy-start(f32[5,4,48,384]{3,2,1,0:T(8,128)} %param.7) | copy-start | bytes 4423684
  1.9 11.5 %collective-permute-start.4 = (f32[5,4,1,384]{3,1,2,0:T(4,128)S(1)}, f32[5,4,1,384]{3,1,2,0:T(4,128)S(1)}, u32[]{:S(2)}, u32[]{:S(2)}) collective-permute-start(f32[5,4,1,384]{3,1,2,0:T(4,128)S(1)} %copy.312), channel_id=1, source_target_pairs={{0,16},{16,32},{32,48},{48,64},{64,80},{80,96},{96,112},{1,17},{17... | collective-permute-start | bytes 92168 | tf_op jit(solution)/shard_map/ppermute | solution.py:21
  6.4 7.0 %collective-permute-start.5 = (f32[5,4,1,384]{3,1,2,0:T(4,128)S(1)}, f32[5,4,1,384]{3,1,2,0:T(4,128)S(1)}, u32[]{:S(2)}, u32[]{:S(2)}) collective-permute-start(f32[5,4,1,384]{3,1,2,0:T(4,128)S(1)} %copy.313), channel_id=1, source_target_pairs={{16,0},{32,16},{48,32},{64,48},{80,64},{96,80},{112,96},{17,1},{33... | collective-permute-start | bytes 92168 | tf_op jit(solution)/shard_map/ppermute | solution.py:23
  14.1 6.1 collective-permute-start.6
  17.6 4.4 collective-permute-start.7
  29.5 32.3 %copy-start.11 = (pred[2080]{0:T(1024)(128)(4,1)S(1)}, pred[2080]{0:T(1024)(128)(4,1)}, u32[]{:S(2)}) copy-start(pred[2080]{0:T(1024)(128)(4,1)} %reshape.332) | copy-start | bytes 6244
  29.5 32.3 %copy-start.12 = (pred[2080]{0:T(1024)(128)(4,1)S(1)}, pred[2080]{0:T(1024)(128)(4,1)}, u32[]{:S(2)}) copy-start(pred[2080]{0:T(1024)(128)(4,1)} %compare_and_fusion) | copy-start | bytes 6244
  103.0 131.8 %all-to-all-start = ((f32[16,1,124800]{2,1,0:T(1,128)}), f32[16,1,124800]{2,1,0:T(1,128)}, u32[]{:S(2)}, u32[]{:S(2)}) async-start(f32[16,1,124800]{2,1,0:T(1,128)} %reshape.367), calls=%async_computation | async-start | bytes 15974400 | tf_op jit(solution)/shard_map/all_to_all | solution.py:147
  312.4 50.8 %all-to-all-start.1 = ((f32[5,4,144,130]{3,1,0,2:T(4,128)}), f32[5,4,144,130]{3,1,0,2:T(4,128)}, u32[]{:S(2)}, u32[]{:S(2)}) async-start(f32[5,4,144,130]{3,1,0,2:T(4,128)} %select_bitcast_fusion.2), calls=%async_computation.1 | async-start | bytes 5898240 | tf_op jit(solution)/shard_map/all_to_all | solution.py:152
  317.6 32.7 %collective-permute-start = (f32[5,4,1,384]{3,1,2,0:T(4,128)S(1)}, f32[5,4,1,384]{3,1,2,0:T(4,128)S(1)}, u32[]{:S(2)}, u32[]{:S(2)}) collective-permute-start(f32[5,4,1,384]{3,1,2,0:T(4,128)S(1)} %copy.310), channel_id=1, source_target_pairs={{0,16},{16,32},{32,48},{48,64},{64,80},{80,96},{96,112},{1,17},{17... | collective-permute-start | bytes 92168 | tf_op jit(solution)/shard_map/ppermute | solution.py:21
  321.2 31.2 %collective-permute-start.1 = (f32[5,4,1,384]{3,1,2,0:T(4,128)S(1)}, f32[5,4,1,384]{3,1,2,0:T(4,128)S(1)}, u32[]{:S(2)}, u32[]{:S(2)}) collective-permute-start(f32[5,4,1,384]{3,1,2,0:T(4,128)S(1)} %copy.311), channel_id=1, source_target_pairs={{16,0},{32,16},{48,32},{64,48},{80,64},{96,80},{112,96},{17,1},{33... | collective-permute-start | bytes 92168 | tf_op jit(solution)/shard_map/ppermute | solution.py:23
  355.1 5.3 collective-permute-start.2
  357.7 4.4 collective-permute-start.3
  379.9 5.4 collective-permute-start.8
  383.4 5.2 collective-permute-start.9
  391.8 6.8 collective-permute-start.10
  396.8 4.7 collective-permute-start.11
  409.0 5.9 collective-permute-start.12
  412.4 5.2 collective-permute-start.13
  420.8 9.0 %collective-permute-start.14 = (f32[5,4,50,1]{2,1,3,0:T(4,128)}, f32[5,4,50,1]{2,1,3,0:T(4,128)}, u32[]{:S(2)}, u32[]{:S(2)}) collective-permute-start(f32[5,4,50,1]{2,1,3,0:T(4,128)} %copy.297), channel_id=1, source_target_pairs={{0,1},{1,2},{2,3},{3,4},{4,5},{5,6},{6,7},{7,8},{8,9},{9,10},{10,1... | collective-permute-start | bytes 12008 | tf_op jit(solution)/shard_map/ppermute | solution.py:21
  427.3 4.7 collective-permute-start.15
  541.1 51.3 %all-to-all-start.2 = ((f32[16,5,4,16,128]{4,3,2,1,0:T(8,128)}), f32[16,5,4,16,128]{4,3,2,1,0:T(8,128)}, u32[]{:S(2)}, u32[]{:S(2)}) async-start(f32[16,5,4,16,128]{4,3,2,1,0:T(8,128)} %fusion.65), calls=%async_computation.2 | async-start | bytes 5242880 | tf_op jit(solution)/shard_map/all_to_all | solution.py:181
  592.4 14.8 %copy-start.13 = (s32[1024]{0:T(1024)S(1)}, s32[1024]{0:T(1024)}, u32[]{:S(2)}) copy-start(s32[1024]{0:T(1024)} %get-tuple-element.40) | copy-start | bytes 12292
  631.8 51.2 %all-to-all-start.3 = ((f32[5,4,128,384]{3,1,0,2:T(4,128)}), f32[5,4,128,384]{3,1,0,2:T(4,128)}, u32[]{:S(2)}, u32[]{:S(2)}) async-start(f32[5,4,128,384]{3,1,0,2:T(4,128)} %bitcast_select_fusion), calls=%async_computation.3 | async-start | bytes 7864320 | tf_op jit(solution)/shard_map/all_to_all | solution.py:185
  (12 other events, 43.4 us)
